TPU v7x, 256 devices: a whole 4x4x8 slice. The times are simulated.
256 devices in a mesh: vocab: 256 (over z, x, y, core).
Axes of the slice: x: 4, y: 4, z: 8, core: 2. Of those that a mesh axis runs over, the one named last changes fastest.
Arguments:
- hidden: bfloat16 [4096, 2560], P('vocab'), may hold values from -3 to 3
- norm_gain: float32 [2560], replicated, may hold values from 0.1 to 1.9
- head: bfloat16 [2560, 73728], P(None, 'vocab'), may hold values from -50 to 50
- token_ids: int32 [4096], P('vocab'), may hold values from 0 to 73447
- req_len: int32 [512], replicated, may hold values from 1 to 8, as said below
- req_owner: int32 [512], replicated, may hold values from 0 to 255, as said below
Outputs:
- logprob: float32 [4096], P('vocab')
- entropy: float32 [4096], P('vocab')
Inputs may be any that keep to these rules, and one draw needn't show every extreme that they name: `req_len`: each device owns exactly 2 requests; the lengths of one device's requests sum to at most 16, and to exactly 16 on some device. `req_owner`: each device index appears exactly 2 times.
All inputs are finite; a program needn't handle non-finite values.
Results may differ from a plain program's by a relative error of at most 0.0037.
Values may be sent and summed in bfloat16 or wider, within the bound.
A program may use at most 128 MiB of HBM per device.

v0:
```python
import jax
import jax.numpy as jnp
from jax import lax
from jax.sharding import PartitionSpec as P

VOCAB_REAL = 73448
EPS = 1e-05
NEG = -1e30
DIGIT = 64


def slice_stats(rows, chosen, head, col_index, real_cols):
    logits = jnp.dot(rows, head, preferred_element_type=jnp.float32) / 10.0
    logits = jnp.where(real_cols[None, :], logits, NEG)
    rowmax = jnp.max(logits, axis=1)
    expo = jnp.where(real_cols[None, :], jnp.exp(logits - rowmax[:, None]), 0.0)
    total = jnp.sum(expo, axis=1)
    weighted = jnp.sum(jnp.where(real_cols[None, :], expo * logits, 0.0), axis=1)
    picked = jnp.sum(jnp.where(col_index[None, :] == chosen[:, None], logits, 0.0), axis=1)
    return (rowmax, total, weighted, picked)


def code_ids(ids):
    digits = [ids // (DIGIT * DIGIT), ids // DIGIT % DIGIT, ids % DIGIT]
    return jnp.stack(digits, axis=1).astype(jnp.bfloat16)


def decode_ids(coded):
    d = coded.astype(jnp.int32)
    return (d[:, 0] * DIGIT + d[:, 1]) * DIGIT + d[:, 2]


def body(hidden, norm_gain, head, token_ids, req_len, req_owner):
    local_rows, width = hidden.shape
    columns = head.shape[1]
    n_dev = lax.axis_size("vocab")
    me = lax.axis_index("vocab")
    values = hidden.astype(jnp.float32)
    scale = lax.rsqrt(jnp.mean(values * values, axis=-1, keepdims=True) + EPS)
    normed = (values * scale * norm_gain[None, :]).astype(jnp.bfloat16)
    packed = jnp.concatenate([normed, code_ids(token_ids)], axis=1)
    col_index = me * columns + jnp.arange(columns, dtype=jnp.int32)
    real_cols = col_index < VOCAB_REAL
    gathered = lax.all_gather(packed, "vocab", axis=0, tiled=True)
    all_rows = gathered[:, :width]
    all_ids = decode_ids(gathered[:, width:])
    rowmax, total, weighted, picked = slice_stats(all_rows, all_ids, head, col_index, real_cols)
    stats = jnp.stack([rowmax, total, weighted, picked], axis=0).reshape(4, n_dev, local_rows)
    stats = jnp.transpose(stats, (1, 0, 2))
    got = lax.all_to_all(stats, "vocab", 0, 0, tiled=True)
    m_i, s_i, w_i, p_i = (got[:, 0], got[:, 1], got[:, 2], got[:, 3])
    top = jnp.max(m_i, axis=0)
    factor = jnp.exp(m_i - top[None, :])
    total_all = jnp.sum(s_i * factor, axis=0)
    weighted_all = jnp.sum(w_i * factor, axis=0)
    picked_all = jnp.sum(p_i, axis=0)
    load = jnp.sum(jnp.where(req_owner == me, req_len, 0))
    live = jnp.arange(local_rows, dtype=jnp.int32) < load
    log_total = jnp.log(total_all)
    logprob = jnp.where(live, picked_all - top - log_total, 0.0)
    entropy = jnp.where(live, top + log_total - weighted_all / total_all, 0.0)
    return (logprob, entropy)


def solution(mesh):
    placed = (P("vocab", None), P(), P(None, "vocab"), P("vocab"), P(), P())
    return jax.shard_map(
        body, mesh=mesh, in_specs=placed, out_specs=(P("vocab"), P("vocab")), check_vma=False
    )
```

profile of v0, /device:TPU:1, one launch (start us, length us, event | category | flops | bytes accessed | tf_op | source)
XLA Modules:
  0.0 206.1 jit_solution(8663673299165401494)
XLA Ops:
  7.2 0.0 copy-start
  7.2 0.0 all-gather.2.cloned.1.call-start
  7.2 0.8 fusion.17
  8.0 0.1 copy.24
  8.1 0.1 copy.25
  8.2 0.1 copy.26
  8.3 1.0 fusion.11
  9.3 1.0 fusion.13
  10.3 0.7 concatenate.5
  11.0 0.0 all-gather.2.cloned.1.call-update
  11.1 137.5 %all-gather.2.cloned.1.call-done = bf16[4096,2563]{1,0:T(8,128)(2,1)} async-done(((bf16[16,2563]{1,0:T(8,128)(2,1)}), bf16[4096,2563]{1,0:T(8,128)(2,1)}) %all-gather.2.cloned.1.call-update) | async-done | bytes 20996112 | tf_op jit(solution)/shard_map/all_gather | solution.py:44
  148.6 1.4 slice_convert_fusion
  150.0 1.7 fusion.9
  151.8 0.0 copy-done
  151.8 12.0 %fusion.20 = (f32[4096]{0:T(1024)S(1)}, f32[4096,288]{0,1:T(8,128)}) fusion(bf16[2560,288]{0,1:T(8,128)(2,1)S(1)} %copy-done, bf16[4096,2563]{1,0:T(8,128)(2,1)} %all-gather.2.cloned.1.call-done, pred[288]{0:T(512)(128)(4,1)S(1)} %broadcast_compare_fusion), kind=kOutput, calls=%fused_computation.49 | convolution fusion | flops 6043332608 | bytes 27181344 | tf_op jit(solution)/shard_map/dot_general | solution.py:13
  163.7 0.0 copy-start.1
  163.8 0.0 copy-start.2
  163.8 0.1 stack.32
  163.8 3.7 %fusion.8 = (f32[4096]{0:T(1024)S(1)}, f32[4096]{0:T(1024)S(1)}, f32[4096]{0:T(1024)S(1)}) fusion(f32[4096,288]{0,1:T(8,128)} %get-tuple-element.17, f32[4096]{0:T(1024)S(1)} %get-tuple-element.16, pred[288]{0:T(512)(128)(4,1)S(1)} %broadcast_compare_fusion, s32[4096]{0:T(1024)S(1)} %fusion.9, s32[288]{0:T(512)S(1)} %iota_add_fusion), kind=kLoop, calls=%fused_computation.7 | loop fusion | flops 10604544 | bytes 4801952 | tf_op jit(solution)/shard_map/reduce_sum | solution.py:17
  167.5 0.1 stack.33
  167.6 0.1 stack.34
  167.7 0.1 stack.35
  167.9 1.1 copy.27
  169.0 8.5 %all-to-all-start = ((f32[256,4,16]{2,1,0:T(4,128)}), f32[256,4,16]{2,1,0:T(4,128)S(1)}, u32[]{:S(2)}, u32[]{:S(2)}) async-start(f32[256,4,16]{2,1,0:T(4,128)} %copy.27), calls=%async_computation | async-start | bytes 1048576 | tf_op jit(solution)/shard_map/all_to_all | solution.py:50
  177.5 0.0 copy-done.1
  177.5 0.0 copy-done.2
  177.5 0.7 select_reduce_fusion.2
  178.2 19.2 %all-to-all-done = f32[256,4,16]{2,1,0:T(4,128)S(1)} async-done(((f32[256,4,16]{2,1,0:T(4,128)}), f32[256,4,16]{2,1,0:T(4,128)S(1)}, u32[]{:S(2)}, u32[]{:S(2)}) %all-to-all-start) | async-done | bytes 65568 | tf_op jit(solution)/shard_map/all_to_all | solution.py:50
  197.5 0.4 fusion.19
  197.9 0.1 reduce_max.19
  197.9 0.1 multiply_reduce_fusion
  198.0 1.2 compare_select_fusion.2
  (4 shorter events, 0.1 us)
Async XLA Ops:
  7.2 144.6 %copy-start = (bf16[2560,288]{0,1:T(8,128)(2,1)S(1)}, bf16[2560,288]{0,1:T(8,128)(2,1)}, u32[]{:S(2)}) copy-start(bf16[2560,288]{0,1:T(8,128)(2,1)} %param.8) | copy-start | bytes 4423684
  7.2 141.4 %all-gather.2.cloned.1.call-start = ((), (), s32[]{:S(2)}) async-start(), calls=%async_computation.1 | async-start | bytes 22106112 | tf_op jit(solution)/shard_map/all_gather | solution.py:44
  163.7 13.8 %copy-start.1 = (s32[512]{0:T(512)S(1)}, s32[512]{0:T(512)}, u32[]{:S(2)}) copy-start(s32[512]{0:T(512)} %param.10) | copy-start | bytes 6148
  163.8 13.8 %copy-start.2 = (s32[512]{0:T(512)S(1)}, s32[512]{0:T(512)}, u32[]{:S(2)}) copy-start(s32[512]{0:T(512)} %param.11) | copy-start | bytes 6148
  169.0 28.5 %all-to-all-start = ((f32[256,4,16]{2,1,0:T(4,128)}), f32[256,4,16]{2,1,0:T(4,128)S(1)}, u32[]{:S(2)}, u32[]{:S(2)}) async-start(f32[256,4,16]{2,1,0:T(4,128)} %copy.27), calls=%async_computation | async-start | bytes 1048576 | tf_op jit(solution)/shard_map/all_to_all | solution.py:50
Sparse Core Ops, SparseCore 0:
  11.9 136.6 all-gather.1
where the time goes:
time: 206 us
  waiting for transfers between devices  157 us (76%)
  between operations  14.1 us (7%)
  other arithmetic  12.1 us (6%)
  matrix products  12 us (6%)
  starting transfers between devices  8.54 us (4%)
  local copies, waits for them, and re-layouts  2.52 us (1%)
    all_gather x1, waiting for transfers between devices, body(): gathered = lax.all_gather(packed, 'vocab', axis=0, tiled=True)  138 us
    all_to_all x1, waiting for transfers between devices, body(): got = lax.all_to_all(stats, 'vocab', 0, 0, tiled=True)  19.2 us
    dot_general x1, matrix products, slice_stats(): logits = jnp.dot(rows, head, preferred_element_type=jnp.float32) / 10.0  12 us
    all_to_all x1, starting transfers between devices, body(): got = lax.all_to_all(stats, 'vocab', 0, 0, tiled=True)  8.5 us
  transfers between devices with their start and end apart: 2, of which 2 were waited for; matrix products, arithmetic and copies ran while one was open for 0% of the time, Pallas kernels for 0%

commit v1 on v0

--- a/solution.py
+++ b/solution.py
@@ -41,7 +41,9 @@
     packed = jnp.concatenate([normed, code_ids(token_ids)], axis=1)
     col_index = me * columns + jnp.arange(columns, dtype=jnp.int32)
     real_cols = col_index < VOCAB_REAL
-    gathered = lax.all_gather(packed, "vocab", axis=0, tiled=True)
+    gathered = jnp.concatenate(
+        lax.all_to_all(jnp.stack([packed] * lax.axis_size("vocab")), "vocab", 0, 0), axis=0
+    )
     all_rows = gathered[:, :width]
     all_ids = decode_ids(gathered[:, width:])
     rowmax, total, weighted, picked = slice_stats(all_rows, all_ids, head, col_index, real_cols)

time: 206 us -> 559 us (2.71)
  waiting for transfers between devices: 157 us -> 497 us
  starting transfers between devices: 8.54 us -> 26.7 us
  between operations: 14.1 us -> 0.76 us
  local copies, waits for them, and re-layouts: 2.52 us -> 9.44 us
    all_to_all x0 -> x1, waiting for transfers between devices: none -> 478 us  [body(): lax.all_to_all(jnp.stack([packed] * lax.axis_size('vocab')), 'vocab', 0, 0)]
    all_gather x1 -> x0, waiting for transfers between devices: 138 us -> none  [body(): gathered = lax.all_gather(packed, 'vocab', axis=0, tiled=True)]
    all_to_all x0 -> x1, starting transfers between devices: none -> 16.5 us  [body(): lax.all_to_all(jnp.stack([packed] * lax.axis_size('vocab')), 'vocab', 0, 0)]
    another operation x0 -> x1, local copies, waits for them, and re-layouts: none -> 7.55 us  [body(): jnp.stack([packed] * lax.axis_size('vocab'))]
where the time goes in v1:
time: 559 us; the launch traced here: 558 us
  waiting for transfers between devices  497 us (89%)
  starting transfers between devices  26.7 us (5%)
  other arithmetic  12.1 us (2%)
  matrix products  12 us (2%)
  local copies, waits for them, and re-layouts  9.44 us (2%)
    all_to_all x1, waiting for transfers between devices, body(): lax.all_to_all(jnp.stack([packed] * lax.axis_size('vocab')), 'vocab', 0, 0)  478 us
    all_to_all x1, waiting for transfers between devices, body(): got = lax.all_to_all(stats, 'vocab', 0, 0, tiled=True)  19.2 us
    all_to_all x1, starting transfers between devices, body(): lax.all_to_all(jnp.stack([packed] * lax.axis_size('vocab')), 'vocab', 0, 0)  16.5 us
    dot_general x1, matrix products, slice_stats(): logits = jnp.dot(rows, head, preferred_element_type=jnp.float32) / 10.0  12 us
  transfers between devices with their start and end apart: 2, of which 2 were waited for; matrix products, arithmetic and copies ran while one was open for 0% of the time, Pallas kernels for 0%

profile of v1, /device:TPU:1, one launch (start us, length us, event | category | flops | bytes accessed | tf_op | source)
XLA Modules:
  0.0 558.4 jit_solution(8116935116390370455)
XLA Ops:
  0.6 0.0 copy-start
  0.6 0.8 fusion.17
  1.4 0.1 copy.28
  1.5 0.1 copy.29
  1.6 0.1 copy.30
  1.7 1.0 fusion.11
  2.8 1.0 fusion.13
  3.7 0.1 concatenate.5
  3.8 7.6 %stack.25 = bf16[256,16,2563]{2,1,0:T(8,128)(2,1)} broadcast(bf16[16,2563]{1,0:T(8,128)(2,1)S(1)} %concatenate.5), dimensions={1,2} | broadcast | bytes 21078112 | tf_op jit(solution)/shard_map/stack | solution.py:45
  11.4 16.5 %all-to-all-start = ((bf16[256,16,2563]{2,1,0:T(8,128)(2,1)}), bf16[256,16,2563]{2,1,0:T(8,128)(2,1)}, u32[]{:S(2)}, u32[]{:S(2)}) async-start(bf16[256,16,2563]{2,1,0:T(8,128)(2,1)} %stack.25), calls=%async_computation | async-start | bytes 44040192 | tf_op jit(solution)/shard_map/all_to_all | solution.py:45
  28.0 478.2 %all-to-all-done = bf16[256,16,2563]{2,1,0:T(8,128)(2,1)} async-done(((bf16[256,16,2563]{2,1,0:T(8,128)(2,1)}), bf16[256,16,2563]{2,1,0:T(8,128)(2,1)}, u32[]{:S(2)}, u32[]{:S(2)}) %all-to-all-start) | async-done | bytes 20996128 | tf_op jit(solution)/shard_map/all_to_all | solution.py:45
  506.2 1.4 slice_convert_fusion
  507.6 1.7 fusion.9
  509.3 0.0 copy-done
  509.4 12.0 %fusion.20 = (f32[4096]{0:T(1024)S(1)}, f32[4096,288]{0,1:T(8,128)}) fusion(bf16[2560,288]{0,1:T(8,128)(2,1)S(1)} %copy-done, bf16[4096,2563]{1,0:T(8,128)(2,1)} %bitcast.3, pred[288]{0:T(512)(128)(4,1)S(1)} %broadcast_compare_fusion), kind=kOutput, calls=%fused_computation.49 | convolution fusion | flops 6043332608 | bytes 27181344 | tf_op jit(solution)/shard_map/dot_general | solution.py:13
  521.3 0.0 copy-start.1
  521.3 0.0 copy-start.2
  521.3 0.1 stack.26
  521.4 3.7 fusion.8
  525.1 0.1 stack.27
  525.2 0.1 stack.28
  525.3 0.1 stack.29
  525.5 1.1 copy.31
  526.6 10.1 %all-to-all-start.1 = ((f32[256,4,16]{2,1,0:T(4,128)}), f32[256,4,16]{2,1,0:T(4,128)S(1)}, u32[]{:S(2)}, u32[]{:S(2)}) async-start(f32[256,4,16]{2,1,0:T(4,128)} %copy.31), calls=%async_computation.1 | async-start | bytes 1048576 | tf_op jit(solution)/shard_map/all_to_all | solution.py:52
  536.7 0.0 copy-done.1
  536.8 0.0 copy-done.2
  536.8 0.7 select_reduce_fusion.2
  537.5 19.2 %all-to-all-done.1 = f32[256,4,16]{2,1,0:T(4,128)S(1)} async-done(((f32[256,4,16]{2,1,0:T(4,128)}), f32[256,4,16]{2,1,0:T(4,128)S(1)}, u32[]{:S(2)}, u32[]{:S(2)}) %all-to-all-start.1) | async-done | bytes 65568 | tf_op jit(solution)/shard_map/all_to_all | solution.py:52
  556.7 0.4 fusion.19
  557.1 0.1 reduce_max.19
  557.2 0.1 multiply_reduce_fusion
  557.2 1.2 compare_select_fusion.2
  (4 shorter events, 0.1 us)
Async XLA Ops:
  0.6 508.7 %copy-start = (bf16[2560,288]{0,1:T(8,128)(2,1)S(1)}, bf16[2560,288]{0,1:T(8,128)(2,1)}, u32[]{:S(2)}) copy-start(bf16[2560,288]{0,1:T(8,128)(2,1)} %param.8) | copy-start | bytes 4423684
  11.4 494.8 %all-to-all-start = ((bf16[256,16,2563]{2,1,0:T(8,128)(2,1)}), bf16[256,16,2563]{2,1,0:T(8,128)(2,1)}, u32[]{:S(2)}, u32[]{:S(2)}) async-start(bf16[256,16,2563]{2,1,0:T(8,128)(2,1)} %stack.25), calls=%async_computation | async-start | bytes 44040192 | tf_op jit(solution)/shard_map/all_to_all | solution.py:45
  521.3 15.4 %copy-start.1 = (s32[512]{0:T(512)S(1)}, s32[512]{0:T(512)}, u32[]{:S(2)}) copy-start(s32[512]{0:T(512)} %param.10) | copy-start | bytes 6148
  521.3 15.4 %copy-start.2 = (s32[512]{0:T(512)S(1)}, s32[512]{0:T(512)}, u32[]{:S(2)}) copy-start(s32[512]{0:T(512)} %param.11) | copy-start | bytes 6148
  526.6 30.1 %all-to-all-start.1 = ((f32[256,4,16]{2,1,0:T(4,128)}), f32[256,4,16]{2,1,0:T(4,128)S(1)}, u32[]{:S(2)}, u32[]{:S(2)}) async-start(f32[256,4,16]{2,1,0:T(4,128)} %copy.31), calls=%async_computation.1 | async-start | bytes 1048576 | tf_op jit(solution)/shard_map/all_to_all | solution.py:52
